TPU v7x, 32 devices: a whole 2x2x4 slice. The times are simulated.
32 devices in a mesh: sample: 8 (over z, y), space: 4 (over x, core).
Axes of the slice: x: 2, y: 2, z: 4, core: 2. Of those that a mesh axis runs over, the one named last changes fastest.
Arguments:
- features: bfloat16 [8, 64, 256, 256], P('sample', 'space'), may hold values from -6 to 6
- weight_one: bfloat16 [3, 3, 256, 256], P(None, None, None, 'sample'), may hold values from -0.125 to 0.125
- offset_one: float32 [256], replicated, may hold values from -0.5 to 0.5
- weight_two: bfloat16 [3, 3, 256, 256], P(None, None, None, 'sample'), may hold values from -0.125 to 0.125
- offset_two: float32 [256], replicated, may hold values from -0.5 to 0.5
Outputs:
- context: bfloat16 [8, 64, 256, 256], P('sample', 'space')
All inputs are finite; a program needn't handle non-finite values.
Results may differ from a plain program's by a relative error of at most 0.0047.
Values may be sent and summed in bfloat16 or wider, within the bound.
A program may use at most 192 MiB of HBM per device.

v0:
```python
import jax
import jax.numpy as jnp
from jax import lax
from jax.sharding import PartitionSpec as P

DILATION_RATE = 8


def extended(block, sides, width):
    for axis, dim in sides:
        count = lax.axis_size(axis)
        forward = [(i, i + 1) for i in range(count - 1)]
        backward = [(target, source) for source, target in forward]
        low = lax.ppermute(
            lax.slice_in_dim(block, block.shape[dim] - width, None, axis=dim), axis, forward
        )
        high = lax.ppermute(lax.slice_in_dim(block, 0, width, axis=dim), axis, backward)
        block = jnp.concatenate([low, block, high], axis=dim)
    return block


def dilated(padded_input, kernel_weights, output_rows):
    tile_width = padded_input.shape[2]
    column_count = jnp.pad(padded_input, ((0, 0), (0, 0), (DILATION_RATE, DILATION_RATE), (0, 0)))
    tap_sum = None
    for row_offset_tap in range(3):
        for column_offset_tap in range(3):
            window = column_count[
                :,
                row_offset_tap * DILATION_RATE : row_offset_tap * DILATION_RATE + output_rows,
                column_offset_tap * DILATION_RATE : column_offset_tap * DILATION_RATE + tile_width,
                :,
            ]
            product = jnp.einsum(
                "shwc,co->shwo",
                window,
                kernel_weights[row_offset_tap, column_offset_tap],
                preferred_element_type=jnp.float32,
            )
            tap_sum = product if tap_sum is None else tap_sum + product
    return tap_sum


def first_layer(padded_input, weight_one, gathered, output_rows):
    gathered = lax.all_gather(weight_one, "sample", axis=3, tiled=True)
    return dilated(padded_input, gathered, output_rows)


def second_layer(padded_input, weight_two, gathered, output_rows):
    gathered = lax.all_gather(weight_two, "sample", axis=3, tiled=True)
    return dilated(padded_input, gathered, output_rows)


def with_rim(feature_values):
    return extended(feature_values, (("space", 1),), DILATION_RATE)


def per_device(features, weight_one, offset_one, weight_two, offset_two):
    rows_dev = features.shape[1]
    kernel_one, kernel_two = (None, None)
    tap_sum = first_layer(with_rim(features), weight_one, kernel_one, rows_dev)
    hidden = jnp.maximum(tap_sum + offset_one, 0.0).astype(jnp.bfloat16)
    hidden_rows = with_rim(hidden)
    result = second_layer(hidden_rows, weight_two, kernel_two, rows_dev)
    return jnp.maximum(result + offset_two, 0.0).astype(jnp.bfloat16)


def solution(mesh):
    return jax.shard_map(
        per_device,
        mesh=mesh,
        in_specs=(
            P("sample", "space", None, None),
            P(None, None, None, "sample"),
            P(),
            P(None, None, None, "sample"),
            P(),
        ),
        out_specs=P("sample", "space", None, None),
        check_vma=False,
    )
```

profile of v0, /device:TPU:1, one launch (start us, length us, event | category | flops | bytes accessed | tf_op | source)
XLA Modules:
  0.0 146.6 jit_solution(10417974059888261316)
XLA Ops:
  7.3 3.1 %fusion.43 = (bf16[1,8,256,256]{3,2,1,0:T(8,128)(2,1)}, bf16[1,8,256,256]{3,2,1,0:T(8,128)(2,1)}) fusion(bf16[1,16,256,256]{3,2,1,0:T(8,128)(2,1)} %param.5), kind=kLoop, calls=%fused_computation.79 | loop fusion | bytes 4194304 | tf_op jit(solution)/shard_map/slice | solution.py:15
  10.4 4.5 %collective-permute-start = (bf16[1,8,256,256]{3,2,1,0:T(8,128)(2,1)}, bf16[1,8,256,256]{3,2,1,0:T(8,128)(2,1)S(1)}, u32[]{:S(2)}, u32[]{:S(2)}) collective-permute-start(bf16[1,8,256,256]{3,2,1,0:T(8,128)(2,1)} %get-tuple-element.7), channel_id=1, source_target_pairs={{0,1},{1,2},{2,3},{4,5},{5,6},{6,7},{8,9},{9,10},{10,11},{12,13},{... | collective-permute-start | bytes 3145736 | tf_op jit(solution)/shard_map/ppermute | solution.py:14
  16.8 10.1 %collective-permute-done = bf16[1,8,256,256]{3,2,1,0:T(8,128)(2,1)S(1)} collective-permute-done((bf16[1,8,256,256]{3,2,1,0:T(8,128)(2,1)}, bf16[1,8,256,256]{3,2,1,0:T(8,128)(2,1)S(1)}, u32[]{:S(2)}, u32[]{:S(2)}) %collective-permute-start) | collective-permute-done | bytes 1048608 | tf_op jit(solution)/shard_map/ppermute | solution.py:14
  26.9 4.7 %collective-permute-done.1 = bf16[1,8,256,256]{3,2,1,0:T(8,128)(2,1)} collective-permute-done((bf16[1,8,256,256]{3,2,1,0:T(8,128)(2,1)}, bf16[1,8,256,256]{3,2,1,0:T(8,128)(2,1)}, u32[]{:S(2)}, u32[]{:S(2)}) %collective-permute-start.1) | collective-permute-done | bytes 1048608 | tf_op jit(solution)/shard_map/ppermute | solution.py:17
  31.6 3.5 %fusion.5 = bf16[1,32,272,256]{3,2,1,0:T(8,128)(2,1)} fusion(bf16[1,8,256,256]{3,2,1,0:T(8,128)(2,1)} %collective-permute-done.1, bf16[1,16,256,256]{3,2,1,0:T(8,128)(2,1)S(1)} %copy-done.1, bf16[1,8,256,256]{3,2,1,0:T(8,128)(2,1)S(1)} %collective-permute-done), kind=kLoop, calls=%fused_computation.9 | loop fusion | flops 26738688 | bytes 8650752 | tf_op jit(solution)/shard_map/concatenate | solution.py:18
  35.1 16.4 %all-gather.3.cloned.1.call-done = bf16[3,3,256,256]{2,3,1,0:T(8,128)(2,1)} async-done(((bf16[3,3,256,32]{2,3,1,0:T(8,128)(2,1)}), bf16[3,3,256,256]{2,3,1,0:T(8,128)(2,1)}) %all-gather.3.cloned.1.call-update) | async-done | bytes 1179664 | tf_op jit(solution)/shard_map/all_gather | solution.py:45
  51.5 4.5 %fusion.25 = f32[16,256,256]{2,1,0:T(8,128)} fusion(bf16[1,32,272,256]{3,2,1,0:T(8,128)(2,1)} %fusion.5, bf16[3,3,256,256]{2,3,1,0:T(8,128)(2,1)} %all-gather.3.cloned.1.call-done), kind=kOutput, calls=%fused_computation.39 | convolution fusion | flops 536870912 | bytes 6422528 | tf_op jit(solution)/shard_map/shwc,co->shwo/dot_general | solution.py:34
  56.1 2.7 %fusion.26 = f32[16,256,256]{2,1,0:T(8,128)} fusion(bf16[1,32,272,256]{3,2,1,0:T(8,128)(2,1)S(1)} %copy-done, bf16[3,3,256,256]{2,3,1,0:T(8,128)(2,1)S(1)} %copy-done.6), kind=kOutput, calls=%fused_computation.41 | convolution fusion | flops 536870912 | bytes 6422528 | tf_op jit(solution)/shard_map/shwc,co->shwo/dot_general | solution.py:34
  58.8 2.7 %fusion.27 = f32[16,256,256]{2,1,0:T(8,128)} fusion(bf16[1,32,272,256]{3,2,1,0:T(8,128)(2,1)S(1)} %copy-done, bf16[3,3,256,256]{2,3,1,0:T(8,128)(2,1)S(1)} %copy-done.6), kind=kOutput, calls=%fused_computation.43 | convolution fusion | flops 536870912 | bytes 6422528 | tf_op jit(solution)/shard_map/shwc,co->shwo/dot_general | solution.py:34
  64.2 2.7 %fusion.33 = f32[16,256,256]{2,1,0:T(8,128)} fusion(bf16[1,32,272,256]{3,2,1,0:T(8,128)(2,1)S(1)} %copy-done, bf16[3,3,256,256]{2,3,1,0:T(8,128)(2,1)S(1)} %copy-done.6), kind=kOutput, calls=%fused_computation.51 | convolution fusion | flops 536870912 | bytes 6422528 | tf_op jit(solution)/shard_map/shwc,co->shwo/dot_general | solution.py:34
  68.9 2.7 %fusion.30 = f32[16,256,256]{2,1,0:T(8,128)} fusion(bf16[1,16,256,256]{3,2,1,0:T(8,128)(2,1)S(1)} %copy-done.1, bf16[1,8,256,256]{3,2,1,0:T(8,128)(2,1)S(1)} %copy-done.3, bf16[3,3,256,256]{2,3,1,0:T(8,128)(2,1)S(1)} %copy-done.6), kind=kOutput, calls=%fused_computation.48 | convolution fusion | flops 537919488 | bytes 7471104 | tf_op jit(solution)/shard_map/shwc,co->shwo/dot_general | solution.py:34
  71.7 2.8 %fusion.34 = f32[16,256,256]{2,1,0:T(8,128)} fusion(bf16[1,16,256,256]{3,2,1,0:T(8,128)(2,1)S(1)} %copy-done.1, bf16[3,3,256,256]{2,3,1,0:T(8,128)(2,1)S(1)} %copy-done.6), kind=kOutput, calls=%fused_computation.52 | convolution fusion | flops 536870912 | bytes 6422528 | tf_op jit(solution)/shard_map/shwc,co->shwo/dot_general | solution.py:34
  74.5 10.8 %maximum_convert_fusion.1 = bf16[16,256,256]{2,1,0:T(8,128)(2,1)S(1)} fusion(f32[16,256,256]{2,1,0:T(8,128)S(1)} %fusion.22, f32[16,256,256]{2,1,0:T(8,128)} %fusion.25, f32[16,256,256]{2,1,0:T(8,128)} %fusion.26, f32[16,256,256]{2,1,0:T(8,128)} %fusion.34, f32[16,256,256]{2,1,0:T(8,128)} %fusion.27, f32[16,256,256]{2,1,0:T(8,128)} %fusion.28, ...), kind=kOutput, calls=%fused_computation.11 | convolution fusion | flops 548405248 | bytes 37880832 | tf_op jit(solution)/shard_map/shwc,co->shwo/dot_general | solution.py:34
  86.8 4.9 %collective-permute-start.2 = (bf16[1,8,256,256]{3,2,1,0:T(8,128)(2,1)}, bf16[1,8,256,256]{3,2,1,0:T(8,128)(2,1)S(1)}, u32[]{:S(2)}, u32[]{:S(2)}) collective-permute-start(bf16[1,8,256,256]{3,2,1,0:T(8,128)(2,1)} %get-tuple-element.5), channel_id=1, source_target_pairs={{0,1},{1,2},{2,3},{4,5},{5,6},{6,7},{8,9},{9,10},{10,11},{12,13},{... | collective-permute-start | bytes 3145736 | tf_op jit(solution)/shard_map/ppermute | solution.py:14
  93.8 3.7 %fusion.37 = f32[16,256,256]{2,1,0:T(8,128)} fusion(bf16[16,256,256]{2,1,0:T(8,128)(2,1)S(1)} %maximum_convert_fusion.1, bf16[3,3,256,256]{2,3,1,0:T(8,128)(2,1)} %all-gather.5.cloned.1.call-done), kind=kOutput, calls=%fused_computation.60 | convolution fusion | flops 536870912 | bytes 6422528 | tf_op jit(solution)/shard_map/shwc,co->shwo/dot_general | solution.py:34
  97.5 6.2 %collective-permute-done.2 = bf16[1,8,256,256]{3,2,1,0:T(8,128)(2,1)S(1)} collective-permute-done((bf16[1,8,256,256]{3,2,1,0:T(8,128)(2,1)}, bf16[1,8,256,256]{3,2,1,0:T(8,128)(2,1)S(1)}, u32[]{:S(2)}, u32[]{:S(2)}) %collective-permute-start.2) | collective-permute-done | bytes 1048608 | tf_op jit(solution)/shard_map/ppermute | solution.py:14
  104.7 3.4 %collective-permute-done.3 = bf16[1,8,256,256]{3,2,1,0:T(8,128)(2,1)} collective-permute-done((bf16[1,8,256,256]{3,2,1,0:T(8,128)(2,1)}, bf16[1,8,256,256]{3,2,1,0:T(8,128)(2,1)}, u32[]{:S(2)}, u32[]{:S(2)}) %collective-permute-start.3) | collective-permute-done | bytes 1048608 | tf_op jit(solution)/shard_map/ppermute | solution.py:17
  110.2 2.7 %fusion.11 = f32[16,256,256]{2,1,0:T(8,128)} fusion(bf16[1,32,272,256]{3,2,1,0:T(8,128)(2,1)S(1)} %select_maximum_fusion, bf16[3,3,256,256]{2,3,1,0:T(8,128)(2,1)S(1)} %copy-done.5), kind=kOutput, calls=%fused_computation.19 | convolution fusion | flops 536870912 | bytes 6422528 | tf_op jit(solution)/shard_map/shwc,co->shwo/dot_general | solution.py:34
  112.9 2.7 %fusion.12 = f32[16,256,256]{2,1,0:T(8,128)} fusion(bf16[1,32,272,256]{3,2,1,0:T(8,128)(2,1)S(1)} %select_maximum_fusion, bf16[3,3,256,256]{2,3,1,0:T(8,128)(2,1)S(1)} %copy-done.5), kind=kOutput, calls=%fused_computation.21 | convolution fusion | flops 536870912 | bytes 6422528 | tf_op jit(solution)/shard_map/shwc,co->shwo/dot_general | solution.py:34
  115.6 2.7 %fusion.13 = f32[16,256,256]{2,1,0:T(8,128)} fusion(bf16[1,32,272,256]{3,2,1,0:T(8,128)(2,1)S(1)} %select_maximum_fusion, bf16[3,3,256,256]{2,3,1,0:T(8,128)(2,1)S(1)} %copy-done.5), kind=kOutput, calls=%fused_computation.23 | convolution fusion | flops 536870912 | bytes 6422528 | tf_op jit(solution)/shard_map/shwc,co->shwo/dot_general | solution.py:34
  118.3 2.7 %fusion.14 = f32[16,256,256]{2,1,0:T(8,128)} fusion(bf16[1,32,272,256]{3,2,1,0:T(8,128)(2,1)S(1)} %select_maximum_fusion, bf16[3,3,256,256]{2,3,1,0:T(8,128)(2,1)S(1)} %copy-done.5), kind=kOutput, calls=%fused_computation.25 | convolution fusion | flops 536870912 | bytes 6422528 | tf_op jit(solution)/shard_map/shwc,co->shwo/dot_general | solution.py:34
  121.0 2.7 %fusion.19 = f32[16,256,256]{2,1,0:T(8,128)} fusion(bf16[1,32,272,256]{3,2,1,0:T(8,128)(2,1)S(1)} %select_maximum_fusion, bf16[3,3,256,256]{2,3,1,0:T(8,128)(2,1)S(1)} %copy-done.5), kind=kOutput, calls=%fused_computation.31 | convolution fusion | flops 536870912 | bytes 6422528 | tf_op jit(solution)/shard_map/shwc,co->shwo/dot_general | solution.py:34
  123.7 4.0 %fusion.8 = f32[16,256,256]{2,1,0:T(8,128)} fusion(bf16[1,8,256,256]{3,2,1,0:T(8,128)(2,1)} %collective-permute-done.3, bf16[1,16,256,256]{3,2,1,0:T(8,128)(2,1)S(1)} %bitcast.172, bf16[3,3,256,256]{2,3,1,0:T(8,128)(2,1)S(1)} %copy-done.5), kind=kOutput, calls=%fused_computation.16 | convolution fusion | flops 537919488 | bytes 7471104 | tf_op jit(solution)/shard_map/shwc,co->shwo/dot_general | solution.py:34
  127.7 12.1 %fusion.36 = bf16[1,16,256,256]{3,2,1,0:T(8,128)(2,1)} fusion(f32[256]{0:T(256)S(1)} %copy-done.8, bf16[1,32,272,256]{3,2,1,0:T(8,128)(2,1)S(1)} %select_maximum_fusion, f32[16,256,256]{2,1,0:T(8,128)} %fusion.8, f32[16,256,256]{2,1,0:T(8,128)} %fusion.11, f32[16,256,256]{2,1,0:T(8,128)} %fusion.12, f32[16,256,256]{2,1,0:T(8,128)} %fusion.37, ...), kind=kOutput, calls=%fused_computation.54 | convolution fusion | flops 548405248 | bytes 37880832 | tf_op jit(solution)/shard_map/shwc,co->shwo/dot_general | solution.py:34
  (30 shorter events, 14.1 us)
Async XLA Ops:
  6.5 25.1 %copy-start.1 = (bf16[1,16,256,256]{3,2,1,0:T(8,128)(2,1)S(1)}, bf16[1,16,256,256]{3,2,1,0:T(8,128)(2,1)}, u32[]{:S(2)}) copy-start(bf16[1,16,256,256]{3,2,1,0:T(8,128)(2,1)} %param.5) | copy-start | bytes 6291460
  6.5 45.0 %all-gather.3.cloned.1.call-start = ((), (), s32[]{:S(2)}) async-start(), calls=%async_computation | async-start | bytes 1327104 | tf_op jit(solution)/shard_map/all_gather | solution.py:45
  7.3 86.6 %all-gather.5.cloned.1.call-start = ((), (), s32[]{:S(2)}) async-start(), calls=%async_computation.1 | async-start | bytes 1327104 | tf_op jit(solution)/shard_map/all_gather | solution.py:50
  10.4 16.5 %collective-permute-start = (bf16[1,8,256,256]{3,2,1,0:T(8,128)(2,1)}, bf16[1,8,256,256]{3,2,1,0:T(8,128)(2,1)S(1)}, u32[]{:S(2)}, u32[]{:S(2)}) collective-permute-start(bf16[1,8,256,256]{3,2,1,0:T(8,128)(2,1)} %get-tuple-element.7), channel_id=1, source_target_pairs={{0,1},{1,2},{2,3},{4,5},{5,6},{6,7},{8,9},{9,10},{10,11},{12,13},{... | collective-permute-start | bytes 3145736 | tf_op jit(solution)/shard_map/ppermute | solution.py:14
  14.9 16.7 %collective-permute-start.1 = (bf16[1,8,256,256]{3,2,1,0:T(8,128)(2,1)}, bf16[1,8,256,256]{3,2,1,0:T(8,128)(2,1)}, u32[]{:S(2)}, u32[]{:S(2)}) collective-permute-start(bf16[1,8,256,256]{3,2,1,0:T(8,128)(2,1)} %get-tuple-element.8), channel_id=1, source_target_pairs={{1,0},{2,1},{3,2},{5,4},{6,5},{7,6},{9,8},{10,9},{11,10},{13,12},{... | collective-permute-start | bytes 3145736 | tf_op jit(solution)/shard_map/ppermute | solution.py:17
  26.9 8.2 %copy-start.2 = (bf16[1,8,256,256]{3,2,1,0:T(8,128)(2,1)}, bf16[1,8,256,256]{3,2,1,0:T(8,128)(2,1)S(1)}, u32[]{:S(2)}) copy-start(bf16[1,8,256,256]{3,2,1,0:T(8,128)(2,1)S(1)} %collective-permute-done) | copy-start | bytes 3145732
  51.5 4.5 %copy-start = (bf16[1,32,272,256]{3,2,1,0:T(8,128)(2,1)S(1)}, bf16[1,32,272,256]{3,2,1,0:T(8,128)(2,1)}, u32[]{:S(2)}) copy-start(bf16[1,32,272,256]{3,2,1,0:T(8,128)(2,1)} %fusion.5) | copy-start | bytes 13369348
  51.5 4.5 %copy-start.6 = (bf16[3,3,256,256]{2,3,1,0:T(8,128)(2,1)S(1)}, bf16[3,3,256,256]{2,3,1,0:T(8,128)(2,1)}, u32[]{:S(2)}) copy-start(bf16[3,3,256,256]{2,3,1,0:T(8,128)(2,1)} %all-gather.3.cloned.1.call-done) | copy-start | bytes 3538948
  66.9 2.1 %copy-start.3 = (bf16[1,8,256,256]{3,2,1,0:T(8,128)(2,1)S(1)}, bf16[1,8,256,256]{3,2,1,0:T(8,128)(2,1)}, u32[]{:S(2)}) copy-start(bf16[1,8,256,256]{3,2,1,0:T(8,128)(2,1)} %copy-done.2) | copy-start | bytes 3145732
  71.7 2.8 %copy-start.7 = (f32[256]{0:T(256)S(1)}, f32[256]{0:T(256)}, u32[]{:S(2)}) copy-start(f32[256]{0:T(256)} %param.7) | copy-start | bytes 3076
  86.8 16.9 %collective-permute-start.2 = (bf16[1,8,256,256]{3,2,1,0:T(8,128)(2,1)}, bf16[1,8,256,256]{3,2,1,0:T(8,128)(2,1)S(1)}, u32[]{:S(2)}, u32[]{:S(2)}) collective-permute-start(bf16[1,8,256,256]{3,2,1,0:T(8,128)(2,1)} %get-tuple-element.5), channel_id=1, source_target_pairs={{0,1},{1,2},{2,3},{4,5},{5,6},{6,7},{8,9},{9,10},{10,11},{12,13},{... | collective-permute-start | bytes 3145736 | tf_op jit(solution)/shard_map/ppermute | solution.py:14
  91.7 16.4 %collective-permute-start.3 = (bf16[1,8,256,256]{3,2,1,0:T(8,128)(2,1)}, bf16[1,8,256,256]{3,2,1,0:T(8,128)(2,1)}, u32[]{:S(2)}, u32[]{:S(2)}) collective-permute-start(bf16[1,8,256,256]{3,2,1,0:T(8,128)(2,1)} %get-tuple-element.6), channel_id=1, source_target_pairs={{1,0},{2,1},{3,2},{5,4},{6,5},{7,6},{9,8},{10,9},{11,10},{13,12},{... | collective-permute-start | bytes 3145736 | tf_op jit(solution)/shard_map/ppermute | solution.py:17
  93.8 9.9 %copy-start.5 = (bf16[3,3,256,256]{2,3,1,0:T(8,128)(2,1)S(1)}, bf16[3,3,256,256]{2,3,1,0:T(8,128)(2,1)}, u32[]{:S(2)}) copy-start(bf16[3,3,256,256]{2,3,1,0:T(8,128)(2,1)} %all-gather.5.cloned.1.call-done) | copy-start | bytes 3538948
  103.7 1.0 copy-start.4
  123.7 4.0 %copy-start.8 = (f32[256]{0:T(256)S(1)}, f32[256]{0:T(256)}, u32[]{:S(2)}) copy-start(f32[256]{0:T(256)} %param.9) | copy-start | bytes 3076
Sparse Core Ops, SparseCore 0:
  9.5 41.9 all-gather.2
  53.7 39.8 all-gather.4
where the time goes:
time: 147 us
  matrix products  67.7 us (46%)
  waiting for transfers between devices  41.6 us (28%)
  starting transfers between devices  13.5 us (9%)
  between operations  13.5 us (9%)
  other arithmetic  5.53 us (4%)
  local copies, waits for them, and re-layouts  4.85 us (3%)
    dot_general x18, matrix products, dilated(): jnp.einsum('shwc,co->shwo', window, kernel_weights[row_offset_tap, column...  67.7 us
    all_gather x1, waiting for transfers between devices, first_layer(): gathered = lax.all_gather(weight_one, 'sample', axis=3, tiled=True)  16.4 us
    ppermute x2, waiting for transfers between devices, extended(): lax.ppermute(lax.slice_in_dim(block, block.shape[dim] - width, None, axis...  16.3 us
    ppermute x2, starting transfers between devices, extended(): lax.ppermute(lax.slice_in_dim(block, block.shape[dim] - width, None, axis...  9.39 us
    ppermute x2, waiting for transfers between devices, extended(): lax.ppermute(lax.slice_in_dim(block, 0, width, axis=dim), axis, backward)  8.11 us
    concatenate x2, other arithmetic, extended(): block = jnp.concatenate([low, block, high], axis=dim)  5.53 us
    slice x2, local copies, waits for them, and re-layouts, extended(): lax.slice_in_dim(block, block.shape[dim] - width, None, axis=dim)  4.59 us
    ppermute x2, starting transfers between devices, extended(): lax.ppermute(lax.slice_in_dim(block, 0, width, axis=dim), axis, backward)  4.02 us
  transfers between devices with their start and end apart: 6, of which 5 were waited for; matrix products, arithmetic and copies ran while one was open for 31% of the time, Pallas kernels for 0%

commit v1 on v0

--- a/solution.py
+++ b/solution.py
@@ -4,6 +4,28 @@
 from jax.sharding import PartitionSpec as P
 
 DILATION_RATE = 8
+
+
+def in_order(parts, dim):
+    parts = jnp.moveaxis(parts, 0, dim)
+    dims = parts.shape
+    return parts.reshape(*dims[:dim], dims[dim] * dims[dim + 1], *dims[dim + 2 :])
+
+
+def gather_around(x, axis, dim):
+    size = lax.axis_size(axis)
+    pairs = [(i, (i + 1) % size) for i in range(size)]
+    back = [(b, a) for a, b in pairs]
+    lower, upper = ([], [])
+    for step in range(size - 1):
+        if step % 2 == 0:
+            lower.append(lax.ppermute(lower[-1] if lower else x, axis, pairs))
+        else:
+            upper.append(lax.ppermute(upper[-1] if upper else x, axis, back))
+    pieces = jnp.stack([*lower[::-1], x, *upper])
+    shift = lax.axis_index(axis) - len(lower)
+    pieces = pieces[(jnp.arange(size) - shift) % size]
+    return in_order(pieces, dim)
 
 
 def extended(block, sides, width):
@@ -42,7 +64,7 @@
 
 
 def first_layer(padded_input, weight_one, gathered, output_rows):
-    gathered = lax.all_gather(weight_one, "sample", axis=3, tiled=True)
+    gathered = gather_around(weight_one, "sample", 3)
     return dilated(padded_input, gathered, output_rows)
 
 

time: 147 us -> 152 us (1.034)
  waiting for transfers between devices: 41.6 us -> 20.8 us
  starting transfers between devices: 13.5 us -> 29 us
  local copies, waits for them, and re-layouts: 4.85 us -> 12.7 us
  matrix products: 67.7 us -> 71.8 us
    all_gather x1 -> x0, waiting for transfers between devices: 16.4 us -> none  [first_layer(): gathered = lax.all_gather(weight_one, 'sample', axis=3, tiled=True)]
    ppermute x0 -> x7, starting transfers between devices: none -> 15 us  [the longest x3 12.9 us: gather_around(): upper.append(lax.ppermute(upper[-1] if upper else x, axis, back))]
    ppermute x0 -> x7, waiting for transfers between devices: none -> 12.8 us  [the longest x4 9.8 us: gather_around(): lower.append(lax.ppermute(lower[-1] if lower else x, axis, pairs))]
    ppermute x2, waiting for transfers between devices: 16.3 us -> 6.21 us  [extended(): lax.ppermute(lax.slice_in_dim(block, block.shape[dim] - width, None, axis...]
    ppermute x2, waiting for transfers between devices: 8.11 us -> 1.72 us  [extended(): lax.ppermute(lax.slice_in_dim(block, 0, width, axis=dim), axis, backward)]
    unnamed x18 -> x19, local copies, waits for them, and re-layouts: 0.26 us -> 5.36 us
    dot_general x18, matrix products: 67.7 us -> 71.8 us  [dilated(): jnp.einsum('shwc,co->shwo', window, kernel_weights[row_offset_tap, column...]
    gather x0 -> x1, local copies, waits for them, and re-layouts: none -> 2.04 us  [gather_around(): pieces = pieces[(jnp.arange(size) - shift) % size]]
  transfers between devices with their start and end apart: 6 -> 12, of which waited for: 5 -> 7; matrix products, arithmetic and copies ran while one was open for 31% -> 37% of each run, Pallas kernels for 0% -> 0%
where the time goes in v1:
time: 152 us
  matrix products  71.8 us (47%)
  starting transfers between devices  29 us (19%)
  waiting for transfers between devices  20.8 us (14%)
  between operations  13.5 us (9%)
  local copies, waits for them, and re-layouts  12.7 us (8%)
  other arithmetic  4.05 us (3%)
    dot_general x18, matrix products, dilated(): jnp.einsum('shwc,co->shwo', window, kernel_weights[row_offset_tap, column...  71.8 us
    ppermute x3, starting transfers between devices, gather_around(): upper.append(lax.ppermute(upper[-1] if upper else x, axis, back))  12.9 us
    ppermute x2, starting transfers between devices, extended(): lax.ppermute(lax.slice_in_dim(block, block.shape[dim] - width, None, axis...  9.98 us
    ppermute x4, waiting for transfers between devices, gather_around(): lower.append(lax.ppermute(lower[-1] if lower else x, axis, pairs))  9.8 us
    ppermute x2, waiting for transfers between devices, extended(): lax.ppermute(lax.slice_in_dim(block, block.shape[dim] - width, None, axis...  6.21 us
    unnamed x19, local copies, waits for them, and re-layouts  5.36 us
    slice x2, local copies, waits for them, and re-layouts, extended(): lax.slice_in_dim(block, block.shape[dim] - width, None, axis=dim)  4.49 us
    concatenate x2, other arithmetic, extended(): block = jnp.concatenate([low, block, high], axis=dim)  4.03 us
  transfers between devices with their start and end apart: 12, of which 7 were waited for; matrix products, arithmetic and copies ran while one was open for 37% of the time, Pallas kernels for 0%

profile of v1, /device:TPU:1, one launch (start us, length us, event | category | flops | bytes accessed | tf_op | source)
XLA Modules:
  0.0 151.8 jit_solution(15144571852403698903)
XLA Ops:
  8.6 6.9 %collective-permute-done.2 = bf16[3,3,256,32]{2,3,1,0:T(8,128)(2,1)S(1)} collective-permute-done((bf16[3,3,256,32]{2,3,1,0:T(8,128)(2,1)}, bf16[3,3,256,32]{2,3,1,0:T(8,128)(2,1)S(1)}, u32[]{:S(2)}, u32[]{:S(2)}) %collective-permute-start.2) | collective-permute-done | bytes 147488 | tf_op jit(solution)/shard_map/ppermute | solution.py:22
  15.5 4.2 %collective-permute-start.6 = (bf16[3,3,256,32]{2,3,1,0:T(8,128)(2,1)}, bf16[3,3,256,32]{2,3,1,0:T(8,128)(2,1)S(1)}, u32[]{:S(2)}, u32[]{:S(2)}) collective-permute-start(bf16[3,3,256,32]{2,3,1,0:T(8,128)(2,1)} %param.6), channel_id=1, source_target_pairs={{4,0},{8,4},{12,8},{16,12},{20,16},{24,20},{28,24},{0,28},{5,1},{9... | collective-permute-start | bytes 442376 | tf_op jit(solution)/shard_map/ppermute | solution.py:24
  22.3 3.0 %fusion.52 = (bf16[1,8,256,256]{3,2,1,0:T(8,128)(2,1)}, bf16[1,8,256,256]{3,2,1,0:T(8,128)(2,1)}) fusion(bf16[1,16,256,256]{3,2,1,0:T(8,128)(2,1)} %param.5), kind=kLoop, calls=%fused_computation.102 | loop fusion | bytes 4194304 | tf_op jit(solution)/shard_map/slice | solution.py:37
  25.3 5.8 %collective-permute-start = (bf16[1,8,256,256]{3,2,1,0:T(8,128)(2,1)}, bf16[1,8,256,256]{3,2,1,0:T(8,128)(2,1)}, u32[]{:S(2)}, u32[]{:S(2)}) collective-permute-start(bf16[1,8,256,256]{3,2,1,0:T(8,128)(2,1)} %get-tuple-element.7), channel_id=1, source_target_pairs={{0,1},{1,2},{2,3},{4,5},{5,6},{6,7},{8,9},{9,10},{10,11},{12,13},{... | collective-permute-start | bytes 3145736 | tf_op jit(solution)/shard_map/ppermute | solution.py:36
  33.1 4.0 %collective-permute-start.7 = (bf16[3,3,256,32]{2,3,1,0:T(8,128)(2,1)S(1)}, bf16[3,3,256,32]{2,3,1,0:T(8,128)(2,1)S(1)}, u32[]{:S(2)}, u32[]{:S(2)}) collective-permute-start(bf16[3,3,256,32]{2,3,1,0:T(8,128)(2,1)S(1)} %collective-permute-done.6), channel_id=1, source_target_pairs={{4,0},{8,4},{12,8},{16,12},{20,16},{24,20},{28,24},{0,28},{5,1},{9... | collective-permute-start | bytes 442376 | tf_op jit(solution)/shard_map/ppermute | solution.py:24
  37.2 2.8 %collective-permute-done.7 = bf16[3,3,256,32]{2,3,1,0:T(8,128)(2,1)S(1)} collective-permute-done((bf16[3,3,256,32]{2,3,1,0:T(8,128)(2,1)S(1)}, bf16[3,3,256,32]{2,3,1,0:T(8,128)(2,1)S(1)}, u32[]{:S(2)}, u32[]{:S(2)}) %collective-permute-start.7) | collective-permute-done | bytes 147488 | tf_op jit(solution)/shard_map/ppermute | solution.py:24
  39.9 4.7 %collective-permute-start.8 = (bf16[3,3,256,32]{2,3,1,0:T(8,128)(2,1)S(1)}, bf16[3,3,256,32]{2,3,1,0:T(8,128)(2,1)S(1)}, u32[]{:S(2)}, u32[]{:S(2)}) collective-permute-start(bf16[3,3,256,32]{2,3,1,0:T(8,128)(2,1)S(1)} %collective-permute-done.7), channel_id=1, source_target_pairs={{4,0},{8,4},{12,8},{16,12},{20,16},{24,20},{28,24},{0,28},{5,1},{9... | collective-permute-start | bytes 442376 | tf_op jit(solution)/shard_map/ppermute | solution.py:24
  52.7 2.7 %fusion.41 = f32[256,16,256]{0,2,1:T(8,128)} fusion(bf16[1,16,256,256]{3,2,1,0:T(8,128)(2,1)S(1)} %copy-done, bf16[3,3,256,256]{2,3,1,0:T(8,128)(2,1)S(1)} %bitcast.210), kind=kOutput, calls=%fused_computation.60 | convolution fusion | flops 536870912 | bytes 6422528 | tf_op jit(solution)/shard_map/shwc,co->shwo/dot_general | solution.py:56
  57.5 2.7 %fusion.32 = f32[16,256,256]{2,1,0:T(8,128)} fusion(bf16[1,32,272,256]{3,2,1,0:T(8,128)(2,1)S(1)} %fusion.5, bf16[3,3,256,256]{2,3,1,0:T(8,128)(2,1)S(1)} %bitcast.211), kind=kOutput, calls=%fused_computation.47 | convolution fusion | flops 536870912 | bytes 6422528 | tf_op jit(solution)/shard_map/shwc,co->shwo/dot_general | solution.py:56
  60.2 2.7 %fusion.33 = f32[16,256,256]{2,1,0:T(8,128)} fusion(bf16[1,32,272,256]{3,2,1,0:T(8,128)(2,1)S(1)} %fusion.5, bf16[3,3,256,256]{2,3,1,0:T(8,128)(2,1)S(1)} %bitcast.212), kind=kOutput, calls=%fused_computation.49 | convolution fusion | flops 536870912 | bytes 6422528 | tf_op jit(solution)/shard_map/shwc,co->shwo/dot_general | solution.py:56
  62.9 2.7 %fusion.34 = f32[16,256,256]{2,1,0:T(8,128)} fusion(bf16[1,32,272,256]{3,2,1,0:T(8,128)(2,1)S(1)} %fusion.5, bf16[3,3,256,256]{2,3,1,0:T(8,128)(2,1)S(1)} %bitcast.213), kind=kOutput, calls=%fused_computation.51 | convolution fusion | flops 536870912 | bytes 6422528 | tf_op jit(solution)/shard_map/shwc,co->shwo/dot_general | solution.py:56
  68.3 2.7 %fusion.40 = f32[16,256,256]{2,1,0:T(8,128)} fusion(bf16[1,32,272,256]{3,2,1,0:T(8,128)(2,1)S(1)} %fusion.5, bf16[3,3,256,256]{2,3,1,0:T(8,128)(2,1)S(1)} %bitcast.215), kind=kOutput, calls=%fused_computation.59 | convolution fusion | flops 536870912 | bytes 6422528 | tf_op jit(solution)/shard_map/shwc,co->shwo/dot_general | solution.py:56
  71.0 3.9 %fusion.37 = f32[16,256,256]{2,1,0:T(8,128)} fusion(bf16[1,16,256,256]{3,2,1,0:T(8,128)(2,1)S(1)} %copy-done, bf16[1,8,256,256]{3,2,1,0:T(8,128)(2,1)} %collective-permute-done, bf16[3,3,256,256]{2,3,1,0:T(8,128)(2,1)S(1)} %bitcast.216), kind=kOutput, calls=%fused_computation.56 | convolution fusion | flops 537919488 | bytes 7471104 | tf_op jit(solution)/shard_map/shwc,co->shwo/dot_general | solution.py:56
  74.9 3.9 %fusion.29 = f32[16,256,256]{2,1,0:T(8,128)} fusion(bf16[1,8,256,256]{3,2,1,0:T(8,128)(2,1)} %collective-permute-done.1, bf16[1,16,256,256]{3,2,1,0:T(8,128)(2,1)S(1)} %copy-done, bf16[3,3,256,256]{2,3,1,0:T(8,128)(2,1)S(1)} %bitcast.217), kind=kOutput, calls=%fused_computation.44 | convolution fusion | flops 537919488 | bytes 7471104 | tf_op jit(solution)/shard_map/shwc,co->shwo/dot_general | solution.py:56
  78.9 11.8 %fusion.12 = bf16[16,256,256]{2,1,0:T(8,128)(2,1)S(1)} fusion(f32[16,256,256]{2,1,0:T(8,128)} %fusion.29, f32[16,256,256]{2,1,0:T(8,128)} %fusion.32, f32[16,256,256]{2,1,0:T(8,128)} %fusion.33, f32[256,16,256]{0,2,1:T(8,128)} %fusion.41, f32[16,256,256]{2,1,0:T(8,128)} %fusion.34, f32[16,256,256]{2,1,0:T(8,128)} %fusion.35, f32[16,256,256]{2,1,0:T(8,128)} %fusion.40, ...), kind=kOutput, calls=%fused_computation.18 | convolution fusion | flops 548405248 | bytes 37880832 | tf_op jit(solution)/shard_map/shwc,co->shwo/dot_general | solution.py:56
  92.1 4.2 %collective-permute-start.9 = (bf16[1,8,256,256]{3,2,1,0:T(8,128)(2,1)}, bf16[1,8,256,256]{3,2,1,0:T(8,128)(2,1)S(1)}, u32[]{:S(2)}, u32[]{:S(2)}) collective-permute-start(bf16[1,8,256,256]{3,2,1,0:T(8,128)(2,1)} %get-tuple-element.5), channel_id=1, source_target_pairs={{0,1},{1,2},{2,3},{4,5},{5,6},{6,7},{8,9},{9,10},{10,11},{12,13},{... | collective-permute-start | bytes 3145736 | tf_op jit(solution)/shard_map/ppermute | solution.py:36
  98.4 3.7 %fusion.44 = f32[16,256,256]{2,1,0:T(8,128)} fusion(bf16[16,256,256]{2,1,0:T(8,128)(2,1)S(1)} %fusion.12, bf16[3,3,256,256]{2,3,1,0:T(8,128)(2,1)} %all-gather.2.cloned.1.call-done), kind=kOutput, calls=%fused_computation.76 | convolution fusion | flops 536870912 | bytes 6422528 | tf_op jit(solution)/shard_map/shwc,co->shwo/dot_general | solution.py:56
  102.1 6.2 %collective-permute-done.9 = bf16[1,8,256,256]{3,2,1,0:T(8,128)(2,1)S(1)} collective-permute-done((bf16[1,8,256,256]{3,2,1,0:T(8,128)(2,1)}, bf16[1,8,256,256]{3,2,1,0:T(8,128)(2,1)S(1)}, u32[]{:S(2)}, u32[]{:S(2)}) %collective-permute-start.9) | collective-permute-done | bytes 1048608 | tf_op jit(solution)/shard_map/ppermute | solution.py:36
  112.7 4.0 %fusion.15 = f32[16,256,256]{2,1,0:T(8,128)} fusion(bf16[1,8,256,256]{3,2,1,0:T(8,128)(2,1)} %collective-permute-done.10, bf16[1,16,256,256]{3,2,1,0:T(8,128)(2,1)S(1)} %bitcast.207, bf16[3,3,256,256]{2,3,1,0:T(8,128)(2,1)S(1)} %copy-done.2), kind=kOutput, calls=%fused_computation.24 | convolution fusion | flops 537919488 | bytes 7471104 | tf_op jit(solution)/shard_map/shwc,co->shwo/dot_general | solution.py:56
  118.6 2.7 %fusion.18 = f32[16,256,256]{2,1,0:T(8,128)} fusion(bf16[1,32,272,256]{3,2,1,0:T(8,128)(2,1)S(1)} %select_maximum_fusion, bf16[3,3,256,256]{2,3,1,0:T(8,128)(2,1)S(1)} %copy-done.2), kind=kOutput, calls=%fused_computation.27 | convolution fusion | flops 536870912 | bytes 6422528 | tf_op jit(solution)/shard_map/shwc,co->shwo/dot_general | solution.py:56
  121.3 2.7 %fusion.19 = f32[16,256,256]{2,1,0:T(8,128)} fusion(bf16[1,32,272,256]{3,2,1,0:T(8,128)(2,1)S(1)} %select_maximum_fusion, bf16[3,3,256,256]{2,3,1,0:T(8,128)(2,1)S(1)} %copy-done.2), kind=kOutput, calls=%fused_computation.29 | convolution fusion | flops 536870912 | bytes 6422528 | tf_op jit(solution)/shard_map/shwc,co->shwo/dot_general | solution.py:56
  126.7 2.7 %fusion.21 = f32[16,256,256]{2,1,0:T(8,128)} fusion(bf16[1,32,272,256]{3,2,1,0:T(8,128)(2,1)S(1)} %select_maximum_fusion, bf16[3,3,256,256]{2,3,1,0:T(8,128)(2,1)S(1)} %copy-done.2), kind=kOutput, calls=%fused_computation.33 | convolution fusion | flops 536870912 | bytes 6422528 | tf_op jit(solution)/shard_map/shwc,co->shwo/dot_general | solution.py:56
  129.4 2.8 %fusion.26 = f32[16,256,256]{2,1,0:T(8,128)} fusion(bf16[1,32,272,256]{3,2,1,0:T(8,128)(2,1)S(1)} %select_maximum_fusion, bf16[3,3,256,256]{2,3,1,0:T(8,128)(2,1)S(1)} %copy-done.2), kind=kOutput, calls=%fused_computation.39 | convolution fusion | flops 536870912 | bytes 6422528 | tf_op jit(solution)/shard_map/shwc,co->shwo/dot_general | solution.py:56
  132.8 12.1 %fusion.43 = bf16[1,16,256,256]{3,2,1,0:T(8,128)(2,1)} fusion(f32[256]{0:T(256)S(1)} %copy-done.5, bf16[1,32,272,256]{3,2,1,0:T(8,128)(2,1)S(1)} %select_maximum_fusion, f32[16,256,256]{2,1,0:T(8,128)} %fusion.15, f32[16,256,256]{2,1,0:T(8,128)} %fusion.18, f32[16,256,256]{2,1,0:T(8,128)} %fusion.19, f32[16,256,256]{2,1,0:T(8,128)} %fusion.44, ...), kind=kOutput, calls=%fused_computation.62 | convolution fusion | flops 548405248 | bytes 37880832 | tf_op jit(solution)/shard_map/shwc,co->shwo/dot_general | solution.py:56
  (47 shorter events, 32.7 us)
Async XLA Ops:
  6.5 41.1 %copy-start.3 = (bf16[3,3,256,32]{2,3,1,0:T(8,128)(2,1)S(1)}, bf16[3,3,256,32]{2,3,1,0:T(8,128)(2,1)}, u32[]{:S(2)}) copy-start(bf16[3,3,256,32]{2,3,1,0:T(8,128)(2,1)} %param.6) | copy-start | bytes 442372
  6.5 91.9 %all-gather.2.cloned.1.call-start = ((), (), s32[]{:S(2)}) async-start(), calls=%async_computation | async-start | bytes 1327104 | tf_op jit(solution)/shard_map/all_gather | solution.py:72
  6.5 9.0 %collective-permute-start.2 = (bf16[3,3,256,32]{2,3,1,0:T(8,128)(2,1)}, bf16[3,3,256,32]{2,3,1,0:T(8,128)(2,1)S(1)}, u32[]{:S(2)}, u32[]{:S(2)}) collective-permute-start(bf16[3,3,256,32]{2,3,1,0:T(8,128)(2,1)} %param.6), channel_id=1, source_target_pairs={{0,4},{4,8},{8,12},{12,16},{16,20},{20,24},{24,28},{28,0},{1,5},{5... | collective-permute-start | bytes 442376 | tf_op jit(solution)/shard_map/ppermute | solution.py:22
  15.5 6.8 %collective-permute-start.3 = (bf16[3,3,256,32]{2,3,1,0:T(8,128)(2,1)S(1)}, bf16[3,3,256,32]{2,3,1,0:T(8,128)(2,1)S(1)}, u32[]{:S(2)}, u32[]{:S(2)}) collective-permute-start(bf16[3,3,256,32]{2,3,1,0:T(8,128)(2,1)S(1)} %collective-permute-done.2), channel_id=1, source_target_pairs={{0,4},{4,8},{8,12},{12,16},{16,20},{20,24},{24,28},{28,0},{1,5},{5... | collective-permute-start | bytes 442376 | tf_op jit(solution)/shard_map/ppermute | solution.py:22
  15.5 17.6 %collective-permute-start.6 = (bf16[3,3,256,32]{2,3,1,0:T(8,128)(2,1)}, bf16[3,3,256,32]{2,3,1,0:T(8,128)(2,1)S(1)}, u32[]{:S(2)}, u32[]{:S(2)}) collective-permute-start(bf16[3,3,256,32]{2,3,1,0:T(8,128)(2,1)} %param.6), channel_id=1, source_target_pairs={{4,0},{8,4},{12,8},{16,12},{20,16},{24,20},{28,24},{0,28},{5,1},{9... | collective-permute-start | bytes 442376 | tf_op jit(solution)/shard_map/ppermute | solution.py:24
  22.3 14.8 %collective-permute-start.4 = (bf16[3,3,256,32]{2,3,1,0:T(8,128)(2,1)S(1)}, bf16[3,3,256,32]{2,3,1,0:T(8,128)(2,1)S(1)}, u32[]{:S(2)}, u32[]{:S(2)}) collective-permute-start(bf16[3,3,256,32]{2,3,1,0:T(8,128)(2,1)S(1)} %collective-permute-done.3), channel_id=1, source_target_pairs={{0,4},{4,8},{8,12},{12,16},{16,20},{20,24},{24,28},{28,0},{1,5},{5... | collective-permute-start | bytes 442376 | tf_op jit(solution)/shard_map/ppermute | solution.py:22
  25.3 30.0 %collective-permute-start = (bf16[1,8,256,256]{3,2,1,0:T(8,128)(2,1)}, bf16[1,8,256,256]{3,2,1,0:T(8,128)(2,1)}, u32[]{:S(2)}, u32[]{:S(2)}) collective-permute-start(bf16[1,8,256,256]{3,2,1,0:T(8,128)(2,1)} %get-tuple-element.7), channel_id=1, source_target_pairs={{0,1},{1,2},{2,3},{4,5},{5,6},{6,7},{8,9},{9,10},{10,11},{12,13},{... | collective-permute-start | bytes 3145736 | tf_op jit(solution)/shard_map/ppermute | solution.py:36
  31.1 24.2 %collective-permute-start.1 = (bf16[1,8,256,256]{3,2,1,0:T(8,128)(2,1)}, bf16[1,8,256,256]{3,2,1,0:T(8,128)(2,1)}, u32[]{:S(2)}, u32[]{:S(2)}) collective-permute-start(bf16[1,8,256,256]{3,2,1,0:T(8,128)(2,1)} %get-tuple-element.8), channel_id=1, source_target_pairs={{1,0},{2,1},{3,2},{5,4},{6,5},{7,6},{9,8},{10,9},{11,10},{13,12},{... | collective-permute-start | bytes 3145736 | tf_op jit(solution)/shard_map/ppermute | solution.py:39
  33.1 6.8 %collective-permute-start.7 = (bf16[3,3,256,32]{2,3,1,0:T(8,128)(2,1)S(1)}, bf16[3,3,256,32]{2,3,1,0:T(8,128)(2,1)S(1)}, u32[]{:S(2)}, u32[]{:S(2)}) collective-permute-start(bf16[3,3,256,32]{2,3,1,0:T(8,128)(2,1)S(1)} %collective-permute-done.6), channel_id=1, source_target_pairs={{4,0},{8,4},{12,8},{16,12},{20,16},{24,20},{28,24},{0,28},{5,1},{9... | collective-permute-start | bytes 442376 | tf_op jit(solution)/shard_map/ppermute | solution.py:24
  37.1 7.8 %collective-permute-start.5 = (bf16[3,3,256,32]{2,3,1,0:T(8,128)(2,1)S(1)}, bf16[3,3,256,32]{2,3,1,0:T(8,128)(2,1)S(1)}, u32[]{:S(2)}, u32[]{:S(2)}) collective-permute-start(bf16[3,3,256,32]{2,3,1,0:T(8,128)(2,1)S(1)} %collective-permute-done.4), channel_id=1, source_target_pairs={{0,4},{4,8},{8,12},{12,16},{16,20},{20,24},{24,28},{28,0},{1,5},{5... | collective-permute-start | bytes 442376 | tf_op jit(solution)/shard_map/ppermute | solution.py:22
  39.9 9.9 %collective-permute-start.8 = (bf16[3,3,256,32]{2,3,1,0:T(8,128)(2,1)S(1)}, bf16[3,3,256,32]{2,3,1,0:T(8,128)(2,1)S(1)}, u32[]{:S(2)}, u32[]{:S(2)}) collective-permute-start(bf16[3,3,256,32]{2,3,1,0:T(8,128)(2,1)S(1)} %collective-permute-done.7), channel_id=1, source_target_pairs={{4,0},{8,4},{12,8},{16,12},{20,16},{24,20},{28,24},{0,28},{5,1},{9... | collective-permute-start | bytes 442376 | tf_op jit(solution)/shard_map/ppermute | solution.py:24
  50.5 2.2 %copy-start = (bf16[1,16,256,256]{3,2,1,0:T(8,128)(2,1)S(1)}, bf16[1,16,256,256]{3,2,1,0:T(8,128)(2,1)}, u32[]{:S(2)}) copy-start(bf16[1,16,256,256]{3,2,1,0:T(8,128)(2,1)} %param.5) | copy-start | bytes 6291460
  74.9 3.9 %copy-start.4 = (f32[256]{0:T(256)S(1)}, f32[256]{0:T(256)}, u32[]{:S(2)}) copy-start(f32[256]{0:T(256)} %param.7) | copy-start | bytes 3076
  92.1 16.2 %collective-permute-start.9 = (bf16[1,8,256,256]{3,2,1,0:T(8,128)(2,1)}, bf16[1,8,256,256]{3,2,1,0:T(8,128)(2,1)S(1)}, u32[]{:S(2)}, u32[]{:S(2)}) collective-permute-start(bf16[1,8,256,256]{3,2,1,0:T(8,128)(2,1)} %get-tuple-element.5), channel_id=1, source_target_pairs={{0,1},{1,2},{2,3},{4,5},{5,6},{6,7},{8,9},{9,10},{10,11},{12,13},{... | collective-permute-start | bytes 3145736 | tf_op jit(solution)/shard_map/ppermute | solution.py:36
  96.3 16.4 %collective-permute-start.10 = (bf16[1,8,256,256]{3,2,1,0:T(8,128)(2,1)}, bf16[1,8,256,256]{3,2,1,0:T(8,128)(2,1)}, u32[]{:S(2)}, u32[]{:S(2)}) collective-permute-start(bf16[1,8,256,256]{3,2,1,0:T(8,128)(2,1)} %get-tuple-element.6), channel_id=1, source_target_pairs={{1,0},{2,1},{3,2},{5,4},{6,5},{7,6},{9,8},{10,9},{11,10},{13,12},{... | collective-permute-start | bytes 3145736 | tf_op jit(solution)/shard_map/ppermute | solution.py:39
  98.4 9.9 %copy-start.2 = (bf16[3,3,256,256]{2,3,1,0:T(8,128)(2,1)S(1)}, bf16[3,3,256,256]{2,3,1,0:T(8,128)(2,1)}, u32[]{:S(2)}) copy-start(bf16[3,3,256,256]{2,3,1,0:T(8,128)(2,1)} %all-gather.2.cloned.1.call-done) | copy-start | bytes 3538948
  129.4 3.4 %copy-start.1 = (f32[16,256,256]{2,1,0:T(8,128)S(1)}, f32[16,256,256]{2,1,0:T(8,128)}, u32[]{:S(2)}) copy-start(f32[16,256,256]{2,1,0:T(8,128)} %fusion.23) | copy-start | bytes 12582916
  129.4 3.4 %copy-start.5 = (f32[256]{0:T(256)S(1)}, f32[256]{0:T(256)}, u32[]{:S(2)}) copy-start(f32[256]{0:T(256)} %param.9) | copy-start | bytes 3076
Sparse Core Ops, SparseCore 0:
  33.2 42.0 all-gather.1
